TPU v7x, 32 devices: a whole 2x2x4 slice. The times are simulated.
32 devices in a mesh: facet: 8 (over y, x, core), slab: 4 (over z).
Axes of the slice: x: 2, y: 2, z: 4, core: 2. Of those that a mesh axis runs over, the one named last changes fastest.
Arguments:
- slab: bfloat16 [2, 8, 4096, 256], P(None, 'facet', 'slab'), may hold values from -6 to 6
- facet_offset: int32 [8], P('facet'), may hold values from 0 to 28672
- subgrid_offset: int32 [8], replicated, may hold values from 0 to 28672
- vis_cell: int32 [4, 8, 32768], P('slab', 'facet'), may hold values from 0 to 16383
- vis_value: float32 [2, 4, 8, 32768], P(None, 'slab', 'facet'), may hold values from -6 to 6
- vis_weight: float32 [4, 8, 32768], P('slab', 'facet'), may hold values from 0.1 to 1
Outputs:
- residual: float32 [2, 4, 512, 256], P(None, 'slab', 'facet')
- facet_update: float32 [2, 8, 4096, 256], P(None, 'facet', 'slab')
All inputs are finite; a program needn't handle non-finite values.
Results may differ from a plain program's by a relative error of at most 0.0041.
Values may be sent and summed in bfloat16 or wider, within the bound.
A program may use at most 64 MiB of HBM per device.

v0:
```python
import math

import jax
import jax.numpy as jnp
from jax import lax
from jax.sharding import PartitionSpec as P

IMAGE = 32768
SG = 256
UVSTEP = 16


def phase_tables(first_row, local_rows, subgrid_offset):
    freq = subgrid_offset[:, None] + UVSTEP * jnp.arange(SG, dtype=jnp.int32)[None, :]
    places = first_row + jnp.arange(local_rows, dtype=jnp.int32)
    turns = (freq % IMAGE)[:, :, None] * (places % IMAGE)[None, None, :] % IMAGE
    angle = turns.astype(jnp.float32) * (2.0 * math.pi / IMAGE)
    return (jnp.cos(angle).astype(jnp.bfloat16), (-jnp.sin(angle)).astype(jnp.bfloat16))


def complex_apply(form, tab_real, tab_imag, slab_real, slab_imag):
    real = jnp.einsum(form, tab_real, slab_real, preferred_element_type=jnp.float32) - jnp.einsum(
        form, tab_imag, slab_imag, preferred_element_type=jnp.float32
    )
    imag = jnp.einsum(form, tab_real, slab_imag, preferred_element_type=jnp.float32) + jnp.einsum(
        form, tab_imag, slab_real, preferred_element_type=jnp.float32
    )
    return jnp.stack([real, imag])


def adjoint_terms(form, tab_real, tab_imag, piece):
    real = jnp.einsum(form, tab_real, piece[0], preferred_element_type=jnp.float32) + jnp.einsum(
        form, tab_imag, piece[1], preferred_element_type=jnp.float32
    )
    imag = jnp.einsum(form, tab_real, piece[1], preferred_element_type=jnp.float32) - jnp.einsum(
        form, tab_imag, piece[0], preferred_element_type=jnp.float32
    )
    return jnp.stack([real, imag])


def body(slab, facet_offset, subgrid_offset, vis_cell, vis_value, vis_weight):
    slabs = lax.axis_size("slab")
    facets = lax.axis_size("facet")
    local_rows = slab.shape[2]
    width = slab.shape[3]
    count_sub = subgrid_offset.shape[0]
    band_rows = SG // slabs
    owned = count_sub * band_rows // facets
    first = facet_offset[0] + lax.axis_index("slab") * local_rows
    tab_real, tab_imag = phase_tables(first, local_rows, subgrid_offset)
    slab_real = slab[0, 0]
    slab_imag = slab[1, 0]
    contrib = complex_apply("skl,lx->skx", tab_real, tab_imag, slab_real, slab_imag)
    banded = lax.psum_scatter(contrib, "slab", scatter_dimension=2, tiled=True)
    banded = banded.reshape(2, count_sub * band_rows, width)
    blocked = lax.psum_scatter(banded, "facet", scatter_dimension=1, tiled=True)
    model = blocked.reshape(2, owned * width) * (1.0 / math.sqrt(local_rows * slabs * facets))
    cells = vis_cell[0, 0]
    weights = vis_weight[0, 0]
    values = vis_value[:, 0, 0]
    gridded = jnp.zeros((2, owned * width), jnp.float32).at[:, cells].add(weights[None, :] * values)
    weight_sum = jnp.zeros((owned * width,), jnp.float32).at[cells].add(weights)
    residual = (gridded - weight_sum[None, :] * model).reshape(2, owned, width)
    sent = residual.astype(jnp.bfloat16)
    columns = lax.all_gather(sent.reshape(2, 1, owned, width), "slab", axis=1, tiled=True)
    flat_real = tab_real.reshape(count_sub * SG, local_rows)
    flat_imag = tab_imag.reshape(count_sub * SG, local_rows)
    piece = lax.all_gather(columns, "facet", axis=2, tiled=True)
    number = piece.shape[2]
    places = jnp.arange(number, dtype=jnp.int32)
    which_sub = places // band_rows
    inner = places % band_rows
    lookup = (
        which_sub[None, :] * SG
        + jnp.arange(slabs, dtype=jnp.int32)[:, None] * band_rows
        + inner[None, :]
    )
    part_real = jnp.take(flat_real, lookup, axis=0)
    part_imag = jnp.take(flat_imag, lookup, axis=0)
    update = adjoint_terms("prl,prx->lx", part_real, part_imag, piece)
    update = update * (1.0 / math.sqrt(count_sub * SG))
    return (residual.reshape(2, 1, owned, width), update.reshape(2, 1, local_rows, width))


def solution(mesh):
    placed = (
        P(None, "facet", "slab", None),
        P("facet"),
        P(),
        P("slab", "facet", None),
        P(None, "slab", "facet", None),
        P("slab", "facet", None),
    )
    return jax.shard_map(
        body,
        mesh=mesh,
        in_specs=placed,
        out_specs=(P(None, "slab", "facet", None), P(None, "facet", "slab", None)),
        check_vma=False,
    )
```

profile of v0, /device:TPU:0, one launch (start us, length us, event | category | flops | bytes accessed | tf_op | source)
XLA Modules:
  0.0 708.6 jit_solution(16114760168823962843)
XLA Ops:
  7.2 0.0 reduce-scatter.3.cloned.1.call-start
  7.9 0.7 broadcast_bitcast_fusion
  8.6 32.1 %fusion.7 = f32[8,256,256]{2,1,0:T(8,128)S(1)} fusion(s32[1024]{0:T(1024)S(1)} %add_select_fusion.5, s32[8,256]{1,0:T(8,128)S(1)} %get-tuple-element.6, bf16[2,1,1024,256]{3,2,1,0:T(8,128)(2,1)} %param.8), kind=kOutput, calls=%fused_computation.27 | convolution fusion | flops 1105199104 | bytes 2633728 | tf_op jit(solution)/shard_map/skl,lx->skx/dot_general | solution.py:25
  40.7 0.0 copy-done.7
  40.8 31.3 %fusion.8 = f32[8,256,256]{2,1,0:T(8,128)S(1)} fusion(s32[1024]{0:T(1024)S(1)} %add_select_fusion.5, s32[8,256]{1,0:T(8,128)S(1)} %get-tuple-element.6, bf16[2,1,1024,256]{3,2,1,0:T(8,128)(2,1)S(1)} %copy-done.7), kind=kOutput, calls=%fused_computation.28 | convolution fusion | flops 1105199104 | bytes 2633728 | tf_op jit(solution)/shard_map/skl,lx->skx/dot_general | solution.py:22
  72.1 31.8 %add_bitcast_fusion = f32[1,8,256,256]{3,2,1,0:T(8,128)S(1)} fusion(f32[8,256,256]{2,1,0:T(8,128)S(1)} %fusion.7, s32[1024]{0:T(1024)S(1)} %add_select_fusion.5, s32[8,256]{1,0:T(8,128)S(1)} %get-tuple-element.6, bf16[2,1,1024,256]{3,2,1,0:T(8,128)(2,1)S(1)} %copy-done.7), kind=kOutput, calls=%fused_computation.44 | convolution fusion | flops 1107820544 | bytes 4730880 | tf_op jit(solution)/shard_map/skl,lx->skx/dot_general | solution.py:25
  103.9 32.2 %subtract_bitcast_fusion = f32[1,8,256,256]{3,2,1,0:T(8,128)S(1)} fusion(f32[8,256,256]{2,1,0:T(8,128)S(1)} %fusion.8, s32[1024]{0:T(1024)S(1)} %add_select_fusion.5, s32[8,256]{1,0:T(8,128)S(1)} %get-tuple-element.6, bf16[2,1,1024,256]{3,2,1,0:T(8,128)(2,1)S(1)} %copy-done.7), kind=kOutput, calls=%fused_computation.45 | convolution fusion | flops 1107820544 | bytes 4730880 | tf_op jit(solution)/shard_map/skl,lx->skx/dot_general | solution.py:22
  136.1 0.0 copy-start.3
  136.1 0.0 copy-start.4
  136.1 0.0 copy-start.5
  136.1 2.4 pad_maximum_fusion
  138.5 0.0 reduce-scatter.3.cloned.1.call-update
  138.5 0.0 reduce-scatter.5.cloned.1.call-start
  138.6 0.0 copy-done.3
  138.6 0.0 copy-done.4
  138.6 0.3 fusion.37
  138.9 79.3 %reduce-scatter.3.cloned.1.call-done = f32[2,8,64,256]{3,2,1,0:T(8,128)} async-done(((f32[2,8,256,256]{3,2,1,0:T(8,128)}), f32[2,8,64,256]{3,2,1,0:T(8,128)}) %reduce-scatter.3.cloned.1.call-update) | async-done | bytes 1048592 | tf_op jit(solution)/shard_map/reduce_scatter | solution.py:54
  218.2 0.0 reduce-scatter.5.cloned.1.call-update
  218.2 0.0 all-gather.2.cloned.1.call-start
  218.2 0.0 copy-done.5
  218.3 0.1 compare_select_fusion
  218.4 8.3 %copy.13 = f32[32768,2]{1,0:T(8,128)} copy(f32[32768,2]{0,1:T(2,128)S(1)} %fusion.37) | data formatting | bytes 524288 | tf_op jit(solution)/shard_map/mul | solution.py:61
  226.7 171.1 %scatter_custom_fusion.1 = f32[16384]{0:T(1024)S(1)} fusion(s32[32768]{0:T(1024)S(1)} %bitcast.79, f32[32768]{0:T(1024)S(1)} %bitcast.78, f32[]{:T(128)} %constant.79.clone.1), kind=kCustom, calls=%fused_computation.68 | custom fusion | flops 32768 | bytes 65540 | tf_op jit(solution)/shard_map/scatter-add | solution.py:62
  397.8 178.0 %scatter_custom_fusion = f32[2,16384]{0,1:T(8,128)} fusion(s32[32768]{0:T(1024)S(1)} %bitcast.80, f32[32768,2]{1,0:T(8,128)} %copy.13, f32[]{:T(128)} %constant.79.clone.1), kind=kCustom, calls=%fused_computation.31 | custom fusion | flops 65536 | bytes 131584 | tf_op jit(solution)/shard_map/scatter-add | solution.py:61
  575.8 0.0 reduce-scatter.5.cloned.1.call-done
  575.8 5.5 copy.14
  581.3 13.3 %fusion.6 = f32[2,16384]{0,1:T(8,128)} fusion(f32[2,16384]{0,1:T(8,128)} %scatter_custom_fusion, f32[2,64,256]{0,2,1:T(8,128)} %copy.14, f32[16384]{0:T(1024)S(1)} %broadcast_multiply_fusion), kind=kLoop, calls=%fused_computation.21 | loop fusion | flops 65536 | bytes 458752 | tf_op jit(solution)/shard_map/sub | solution.py:63
  594.6 5.2 copy.18
  599.9 15.1 %all_gather.6 = bf16[2,4,64,256]{3,2,1,0:T(8,128)(2,1)} all-gather(bf16[2,1,64,256]{3,2,1,0:T(8,128)(2,1)S(1)} %convert_element_type.34), channel_id=1, replica_groups=mesh['facet'=8,'slab'=4] {'slab'}, dimensions={1}, use_global_device_ids=true | all-gather | bytes 327680 | tf_op jit(solution)/shard_map/all_gather | solution.py:65
  615.0 0.0 all-gather.2.cloned.1.call-update
  615.1 0.1 fusion.42
  615.2 36.1 %cosine_convert_fusion = (bf16[2048,1024]{1,0:T(8,128)(2,1)}, bf16[2048,1024]{1,0:T(8,128)(2,1)}) fusion(s32[1024]{0:T(1024)S(1)} %add_select_fusion.5, s32[2048]{0:T(1024)S(1)} %add_select_fusion.3), kind=kLoop, calls=%fused_computation.23 | loop fusion | flops 35651584 | bytes 8400896 | tf_op jit(solution)/shard_map/convert_element_type | solution.py:18
  651.2 13.7 %gather_fusion.1 = bf16[2048,1024]{1,0:T(8,128)(2,1)} fusion(bf16[2048,1024]{1,0:T(8,128)(2,1)} %get-tuple-element.4, s32[2048]{0:T(1024)S(1)} %broadcast_clamp_fusion), kind=kCustom, calls=%fused_computation.1.clone | custom fusion | bytes 8396800 | tf_op jit(solution)/shard_map/jit(_take)/gather | solution.py:79
  665.0 6.2 copy.17
  671.2 13.7 %gather_fusion = bf16[2048,1024]{1,0:T(8,128)(2,1)} fusion(bf16[2048,1024]{1,0:T(8,128)(2,1)} %get-tuple-element.3, s32[2048]{0:T(1024)S(1)} %broadcast_clamp_fusion), kind=kCustom, calls=%fused_computation.clone | custom fusion | bytes 8396800 | tf_op jit(solution)/shard_map/jit(_take)/gather | solution.py:78
  684.9 6.3 copy.16
  691.1 0.1 compare_and_fusion
  691.2 0.0 all-gather.2.cloned.1.call-done
  691.2 0.0 copy-start
  691.3 0.0 copy-start.6
  691.3 3.9 fusion.22
  695.2 0.0 copy-done
  695.2 0.5 copy-done.6
  695.7 1.2 fusion.21
  696.9 0.9 copy-done.1
  697.9 1.2 fusion.26
  699.1 1.2 fusion.28
  700.4 1.5 maximum_multiply_fusion
  (15 shorter events, 0.1 us)
Async XLA Ops:
  7.2 211.0 %reduce-scatter.3.cloned.1.call-start = ((), (), s32[]{:S(2)}) async-start(), calls=%async_computation.2 | async-start | bytes 5242880 | tf_op jit(solution)/shard_map/reduce_scatter | solution.py:54
  8.6 32.1 %copy-start.7 = (bf16[2,1,1024,256]{3,2,1,0:T(8,128)(2,1)S(1)}, bf16[2,1,1024,256]{3,2,1,0:T(8,128)(2,1)}, u32[]{:S(2)}) copy-start(bf16[2,1,1024,256]{3,2,1,0:T(8,128)(2,1)} %param.8) | copy-start | bytes 3145732
  136.1 2.5 copy-start.3
  136.1 2.5 copy-start.4
  136.1 82.1 %copy-start.5 = (s32[1,1,32768]{2,1,0:T(1,128)S(1)}, s32[1,1,32768]{2,1,0:T(1,128)}, u32[]{:S(2)}) copy-start(s32[1,1,32768]{2,1,0:T(1,128)} %param.11) | copy-start | bytes 393220
  138.5 437.3 %reduce-scatter.5.cloned.1.call-start = ((), (), s32[]{:S(2)}) async-start(), calls=%async_computation.3 | async-start | bytes 1179648 | tf_op jit(solution)/shard_map/reduce_scatter | solution.py:56
  218.2 473.0 %all-gather.2.cloned.1.call-start = ((), (), s32[]{:S(2)}) async-start(), calls=%async_computation.4 | async-start | bytes 2359296 | tf_op jit(solution)/shard_map/all_gather | solution.py:68
  599.8 65.2 %copy-start.2 = (f32[2,1,64,256]{3,2,1,0:T(8,128)}, f32[2,1,64,256]{3,2,1,0:T(8,128)S(1)}, u32[]{:S(2)}) copy-start(f32[2,1,64,256]{3,2,1,0:T(8,128)S(1)} %copy.18) | copy-start | bytes 393220
  691.2 3.9 copy-start
  691.3 4.4 copy-start.6
  695.7 2.2 copy-start.1
Sparse Core Ops, SparseCore 0:
  138.6 79.5 reduce-scatter.2
  221.3 36.4 reduce-scatter.4
  615.1 27.7 all-gather.1
where the time goes:
time: 721 us; the launch traced here: 709 us
  other arithmetic  404 us (56%)
  matrix products  135 us (19%)
  waiting for transfers between devices  79.4 us (11%)
  local copies, waits for them, and re-layouts  60.5 us (8%)
  blocking collectives  15.1 us (2%)
  between operations  14.9 us (2%)
    scatter-add x1, other arithmetic, body(): jnp.zeros((2, owned * width), jnp.float32).at[:, cells]  178 us
    scatter-add x1, other arithmetic, body(): weight_sum = jnp.zeros((owned * width,), jnp.float32).at[cells].add(weights)  171 us
    reduce_scatter x1, waiting for transfers between devices, body(): banded = lax.psum_scatter(contrib, 'slab', scatter_dimension=2, tiled=True)  79.3 us
    convert_element_type x1, other arithmetic, phase_tables(): jnp.cos(angle).astype(jnp.bfloat16)  36.1 us
    dot_general x1, matrix products, complex_apply(): jnp.einsum(form, tab_imag, slab_imag, preferred_element_type=jnp.float32)  32.2 us
    dot_general x1, matrix products, complex_apply(): jnp.einsum(form, tab_real, slab_imag, preferred_element_type=jnp.float32)  32.1 us
    dot_general x1, matrix products, complex_apply(): jnp.einsum(form, tab_imag, slab_real, preferred_element_type=jnp.float32)  31.8 us
    dot_general x1, matrix products, complex_apply(): jnp.einsum(form, tab_real, slab_real, preferred_element_type=jnp.float32)  31.3 us
  transfers between devices with their start and end apart: 3, of which 1 were waited for; matrix products, arithmetic and copies ran while one was open for 61% of the time, Pallas kernels for 0%

commit v1 on v0

v1 whole, which is shorter than its diff:
```python
import functools
import math

import jax
import jax.numpy as jnp
from jax import lax
from jax.experimental import pallas as pl
from jax.experimental.pallas import tpu as pltpu
from jax.sharding import PartitionSpec as P

IMAGE = 32768
SG = 256
UVSTEP = 16
F32 = jnp.float32
BF16 = jnp.bfloat16


def cis(turns):
    turns = turns & (IMAGE - 1)
    quarter = IMAGE // 4
    quad = (turns + quarter // 2) // quarter if quarter & (quarter - 1) else lax.shift_right_logical(
        turns + quarter // 2, quarter.bit_length() - 1
    )
    t = (turns - quad * quarter).astype(F32) * (2.0 * math.pi / IMAGE)
    z = t * t
    s = ((-1.9515295891e-4 * z + 8.3321608736e-3) * z - 1.6666654611e-1) * z * t + t
    c = ((2.443315711809948e-5 * z - 1.388731625493765e-3) * z + 4.166664568298827e-2) * z * z - 0.5 * z + 1.0
    odd = (quad & 1) == 1
    cos = jnp.where(odd, s, c)
    sin = jnp.where(odd, c, s)
    cos = jnp.where(((quad + 1) & 2) == 2, -cos, cos)
    sin = jnp.where((quad & 2) == 2, -sin, sin)
    return cos, sin


def grid_kernel(width, rows, cell_ref, value_ref, weight_ref, out_ref):
    @pl.when(pl.program_id(0) == 0)
    def _():
        out_ref[...] = jnp.zeros_like(out_ref)

    cell = cell_ref[...]
    weight = weight_ref[...]
    chunk = cell.shape[1]
    row = lax.shift_right_logical(cell, width.bit_length() - 1)
    col = cell & (width - 1)
    hot = jnp.where(lax.broadcasted_iota(jnp.int32, (width, chunk), 0) == col, 1.0, 0.0).astype(BF16)
    mine = lax.broadcasted_iota(jnp.int32, (rows, chunk), 0) == row
    terms = [weight * value_ref[0:1, :], weight * value_ref[1:2, :], weight]
    left = jnp.concatenate([jnp.where(mine, t, 0.0).astype(BF16) for t in terms], axis=0)
    out_ref[...] += lax.dot_general(left, hot, (((1,), (1,)), ((), ())), preferred_element_type=F32)


def grid_visibilities(cells, values, weights, owned, width):
    count = cells.shape[1]
    rows = -(-owned // 16) * 16
    chunk = min(count, 2048)
    out = pl.pallas_call(
        functools.partial(grid_kernel, width, rows),
        grid=(count // chunk,),
        in_specs=[
            pl.BlockSpec((1, chunk), lambda i: (0, i)),
            pl.BlockSpec((2, chunk), lambda i: (0, i)),
            pl.BlockSpec((1, chunk), lambda i: (0, i)),
        ],
        out_specs=pl.BlockSpec((3 * rows, width), lambda i: (0, 0)),
        out_shape=jax.ShapeDtypeStruct((3 * rows, width), F32),
        cost_estimate=pl.CostEstimate(flops=6 * rows * width * count, bytes_accessed=16 * count, transcendentals=0),
        name="gridding",
    )(cells, values, weights)
    return out.reshape(3, rows, width)[:, :owned]


def forward_kernel(first_ref, subs_ref, slab_ref, out_ref, cos_ref, sin_ref):
    s = pl.program_id(0)
    rows, local = cos_ref.shape
    first = first_ref[0]

    @pl.when(s == 0)
    def _():
        k = lax.broadcasted_iota(jnp.int32, (rows, local), 0)
        y = lax.broadcasted_iota(jnp.int32, (rows, local), 1) + first
        c, n = cis((UVSTEP * k) * y)
        cos_ref[...] = c
        sin_ref[...] = n

    y = lax.broadcasted_iota(jnp.int32, (8, local), 1) + first
    c1, s1 = cis(subs_ref[s] * y)
    c1, s1 = c1[0:1], s1[0:1]
    c2, s2 = cos_ref[...], sin_ref[...]
    tab_real = (c1 * c2 - s1 * s2).astype(BF16)
    tab_imag = (-(s1 * c2 + c1 * s2)).astype(BF16)
    re, im = slab_ref[0], slab_ref[1]
    dot = functools.partial(jnp.dot, preferred_element_type=F32)
    real = dot(tab_real, re) - dot(tab_imag, im)
    imag = dot(tab_real, im) + dot(tab_imag, re)
    slabs, band = out_ref.shape[1], out_ref.shape[3]
    for p in range(slabs):
        out_ref[0, p, 0] = real[p * band:(p + 1) * band].astype(out_ref.dtype)
        out_ref[1, p, 0] = imag[p * band:(p + 1) * band].astype(out_ref.dtype)


def forward(first, subs, slab, slabs):
    _, local, width = slab.shape
    count = subs.shape[0]
    band = SG // slabs
    return pl.pallas_call(
        forward_kernel,
        grid=(count,),
        in_specs=[
            pl.BlockSpec(memory_space=pltpu.SMEM),
            pl.BlockSpec(memory_space=pltpu.SMEM),
            pl.BlockSpec((2, local, width), lambda s: (0, 0, 0)),
        ],
        out_specs=pl.BlockSpec((2, slabs, 1, band, width), lambda s: (0, 0, s, 0, 0)),
        out_shape=jax.ShapeDtypeStruct((2, slabs, count, band, width), BF16),
        scratch_shapes=[pltpu.VMEM((SG, local), F32), pltpu.VMEM((SG, local), F32)],
        name="forward",
    )(first, subs, slab)


def adjoint_kernel(scale, slabs, first_ref, subs_ref, sent_ref, out_ref):
    tile = out_ref.shape[1]
    count = subs_ref.shape[1]
    band = SG // slabs
    start = first_ref[0] + pl.program_id(0) * tile
    yk = lax.broadcasted_iota(jnp.int32, (tile, SG), 0) + start
    c2, s2 = cis((UVSTEP * lax.broadcasted_iota(jnp.int32, (tile, SG), 1)) * yk)
    ys = lax.broadcasted_iota(jnp.int32, (tile, count), 0) + start
    c1, s1 = cis(ys * subs_ref[...])
    real = jnp.zeros(out_ref.shape[1:], F32)
    imag = jnp.zeros(out_ref.shape[1:], F32)
    dot = functools.partial(jnp.dot, preferred_element_type=F32)
    for s in range(count):
        a, b = c1[:, s:s + 1], s1[:, s:s + 1]
        tab_real = (a * c2 - b * s2).astype(BF16)
        tab_imag = (-(b * c2 + a * s2)).astype(BF16)
        re = jnp.concatenate([sent_ref[0, p, s] for p in range(slabs)], axis=0)
        im = jnp.concatenate([sent_ref[1, p, s] for p in range(slabs)], axis=0)
        real += dot(tab_real, re) + dot(tab_imag, im)
        imag += dot(tab_real, im) - dot(tab_imag, re)
    out_ref[0] = real * scale
    out_ref[1] = imag * scale


def adjoint(first, subs, sent, local):
    _, slabs, count, band, width = sent.shape
    tile = min(local, 256)
    return pl.pallas_call(
        functools.partial(adjoint_kernel, 1.0 / math.sqrt(count * SG), slabs),
        grid=(local // tile,),
        in_specs=[
            pl.BlockSpec(memory_space=pltpu.SMEM),
            pl.BlockSpec((1, count), lambda i: (0, 0)),
            pl.BlockSpec((2, slabs, count, band, width), lambda i: (0, 0, 0, 0, 0)),
        ],
        out_specs=pl.BlockSpec((2, tile, width), lambda i: (0, i, 0)),
        out_shape=jax.ShapeDtypeStruct((2, local, width), F32),
        name="adjoint",
    )(first, subs[None, :], sent)


def body(slab, facet_offset, subgrid_offset, vis_cell, vis_value, vis_weight):
    slabs = lax.axis_size("slab")
    facets = lax.axis_size("facet")
    local_rows = slab.shape[2]
    width = slab.shape[3]
    count_sub = subgrid_offset.shape[0]
    band = SG // slabs
    owned = count_sub * band // facets
    first = (facet_offset + lax.axis_index("slab") * local_rows).astype(jnp.int32)
    sums = grid_visibilities(vis_cell[0], vis_value[:, 0, 0], vis_weight[0], owned, width)
    contrib = forward(first, subgrid_offset, slab[:, 0], slabs)
    contrib = contrib.reshape(2, slabs, facets, owned, width)
    parts = lax.all_to_all(contrib, "facet", 2, 2, tiled=True)
    parts = jnp.sum(parts, axis=2, dtype=F32).astype(BF16)
    parts = lax.all_to_all(parts, "slab", 1, 1, tiled=True)
    scale = 1.0 / math.sqrt(local_rows * slabs * facets)
    model = jnp.sum(parts, axis=1, dtype=F32) * scale
    residual = sums[:2] - sums[2:] * model
    sent = residual.astype(BF16).reshape(2, 1, 1, owned, width)
    piece = lax.all_gather(sent, "slab", axis=1, tiled=True)
    piece = lax.all_gather(piece, "facet", axis=2, tiled=True)
    piece = piece.reshape(2, slabs, count_sub, band, width)
    update = adjoint(first, subgrid_offset, piece, local_rows)
    return (residual.reshape(2, 1, owned, width), update.reshape(2, 1, local_rows, width))


def solution(mesh):
    placed = (
        P(None, "facet", "slab", None),
        P("facet"),
        P(),
        P("slab", "facet", None),
        P(None, "slab", "facet", None),
        P("slab", "facet", None),
    )
    return jax.shard_map(
        body,
        mesh=mesh,
        in_specs=placed,
        out_specs=(P(None, "slab", "facet", None), P(None, "facet", "slab", None)),
        check_vma=False,
    )
```

time: 721 us -> 132 us (0.18); the launches traced: 709 us -> 131 us
  other arithmetic: 404 us -> 1.96 us
  matrix products: 135 us -> 0 us
  local copies, waits for them, and re-layouts: 60.5 us -> 5.7 us
  Pallas kernels: 0 us -> 30.9 us
  waiting for transfers between devices: 79.4 us -> 52.1 us
  starting transfers between devices: 0.12 us -> 10.2 us
    scatter-add x2 -> x0, other arithmetic: 349 us -> none  [the longest x1 178 us: body(): jnp.zeros((2, owned * width), jnp.float32).at[:, cells]]
    dot_general x8 -> x0, matrix products: 135 us -> none  [the longest x1 32.2 us: complex_apply(): jnp.einsum(form, tab_imag, slab_imag, preferred_element_type=jnp.float32)]
    reduce_scatter x2 -> x0, waiting for transfers between devices: 79.3 us -> none  [the longest x1 79.3 us: body(): banded = lax.psum_scatter(contrib, 'slab', scatter_dimension=2, tiled=True)]
    gather x4 -> x0, local copies, waits for them, and re-layouts: 39.9 us -> none  [the longest x2 20 us: body(): part_real = jnp.take(flat_real, lookup, axis=0)]
    convert_element_type x2 -> x1, other arithmetic: 36.1 us -> 0.02 us  [body(): sent = residual.astype(BF16).reshape(2, 1, 1, owned, width)]
    pallas_call x0 -> x3, Pallas kernels: none -> 30.9 us  [the longest x1 11.2 us: grid_visibilities(): pl.pallas_call(functools.partial(grid_kernel, width, rows), grid=(count /...]
    all_gather x1, waiting for transfers between devices: 0.01 us -> 26.4 us  [body(): piece = lax.all_gather(piece, 'facet', axis=2, tiled=True)]
    all_to_all x0 -> x2, waiting for transfers between devices: none -> 25.7 us  [the longest x1 25.7 us: body(): parts = lax.all_to_all(contrib, 'facet', 2, 2, tiled=True)]
  transfers between devices with their start and end apart: 3 -> 3, of which waited for: 1 -> 2; matrix products, arithmetic and copies ran while one was open for 61% -> 3% of each run, Pallas kernels for 0% -> 9%
where the time goes in v1:
time: 132 us; the launch traced here: 131 us
  waiting for transfers between devices  52.1 us (39%)
  Pallas kernels  30.9 us (23%)
  blocking collectives  15.7 us (12%)
  between operations  14.7 us (11%)
  starting transfers between devices  10.2 us (8%)
  local copies, waits for them, and re-layouts  5.7 us (4%)
  other arithmetic  1.96 us (1%)
    all_gather x1, waiting for transfers between devices, body(): piece = lax.all_gather(piece, 'facet', axis=2, tiled=True)  26.4 us
    all_to_all x1, waiting for transfers between devices, body(): parts = lax.all_to_all(contrib, 'facet', 2, 2, tiled=True)  25.7 us
    all_gather x1, blocking collectives, body(): piece = lax.all_gather(sent, 'slab', axis=1, tiled=True)  15.7 us
    pallas_call x1, Pallas kernels, grid_visibilities(): pl.pallas_call(functools.partial(grid_kernel, width, rows), grid=(count /...  11.2 us
    pallas_call x1, Pallas kernels, forward(): pl.pallas_call(forward_kernel, grid=(count,), in_specs=[pl.BlockSpec(memo...  10 us
    pallas_call x1, Pallas kernels, adjoint(): pl.pallas_call(functools.partial(adjoint_kernel, 1.0 / math.sqrt(count *...  9.67 us
    all_to_all x1, starting transfers between devices, body(): parts = lax.all_to_all(contrib, 'facet', 2, 2, tiled=True)  5.33 us
    all_to_all x1, starting transfers between devices, body(): parts = lax.all_to_all(parts, 'slab', 1, 1, tiled=True)  4.87 us
  transfers between devices with their start and end apart: 3, of which 2 were waited for; matrix products, arithmetic and copies ran while one was open for 3% of the time, Pallas kernels for 9%

profile of v1, /device:TPU:0, one launch (start us, length us, event | category | flops | bytes accessed | tf_op | source)
XLA Modules:
  0.0 131.3 jit_solution(39923641225212671)
XLA Ops:
  7.8 10.0 %forward.1 = bf16[2,4,8,64,256]{4,3,2,1,0:T(8,128)(2,1)} custom-call(s32[1]{0:T(128)S(6)} %add.7.first_ref, s32[8]{0:T(128)} %subs_ref.1, bf16[2,1024,256]{2,1,0:T(8,128)(2,1)} %bitcast.30), custom_call_target="tpu_custom_call" | custom-call | tf_op jit(solution)/shard_map/forward/pallas_call | solution.py:106
  17.9 3.2 %copy.13 = bf16[2,4,8,64,256]{4,3,1,0,2:T(8,128)(2,1)} copy(bf16[2,4,8,64,256]{4,3,2,1,0:T(8,128)(2,1)} %forward.1) | data formatting | bytes 4194304 | tf_op jit(solution)/shard_map/forward/pallas_call | solution.py:106
  21.0 0.0 copy-start
  21.0 5.3 %all-to-all-start = ((bf16[2,4,8,64,256]{4,3,1,0,2:T(8,128)(2,1)}), bf16[2,4,8,64,256]{4,3,1,0,2:T(8,128)(2,1)S(1)}, u32[]{:S(2)}, u32[]{:S(2)}) async-start(bf16[2,4,8,64,256]{4,3,1,0,2:T(8,128)(2,1)} %copy.13), calls=%async_computation | async-start | bytes 4194304 | tf_op jit(solution)/shard_map/all_to_all | solution.py:174
  26.4 0.0 copy-done
  26.4 0.9 copy.19
  27.3 25.7 %all-to-all-done = bf16[2,4,8,64,256]{4,3,1,0,2:T(8,128)(2,1)S(1)} async-done(((bf16[2,4,8,64,256]{4,3,1,0,2:T(8,128)(2,1)}), bf16[2,4,8,64,256]{4,3,1,0,2:T(8,128)(2,1)S(1)}, u32[]{:S(2)}, u32[]{:S(2)}) %all-to-all-start) | async-done | bytes 2097184 | tf_op jit(solution)/shard_map/all_to_all | solution.py:174
  53.0 0.4 reduce_sum.25
  53.4 0.7 copy.14
  54.1 4.9 %all-to-all-start.1 = ((bf16[2,4,64,256]{3,2,0,1:T(8,128)(2,1)}), bf16[2,4,64,256]{3,2,0,1:T(8,128)(2,1)S(1)}, u32[]{:S(2)}, u32[]{:S(2)}) async-start(bf16[2,4,64,256]{3,2,0,1:T(8,128)(2,1)} %copy.14), calls=%async_computation.1 | async-start | bytes 524288 | tf_op jit(solution)/shard_map/all_to_all | solution.py:176
  58.9 0.0 all-gather.2.cloned.1.call-start
  59.0 11.2 %gridding.1 = f32[192,256]{1,0:T(8,128)} custom-call(s32[1,32768]{1,0:T(1,128)} %bitcast.33, f32[2,32768]{1,0:T(2,128)} %bitcast.31, f32[1,32768]{1,0:T(1,128)} %bitcast.34), custom_call_target="tpu_custom_call" | custom-call | flops 3221225472 | bytes 524288 | tf_op jit(solution)/shard_map/gridding/pallas_call | solution.py:57
  70.2 0.9 slice.16
  71.1 0.8 slice_multiply_fusion
  71.9 0.0 all-to-all-done.1
  72.0 15.7 %all_gather.6 = bf16[2,4,1,64,256]{4,3,2,1,0:T(8,128)(2,1)} all-gather(bf16[2,1,1,64,256]{4,3,2,1,0:T(8,128)(2,1)S(1)} %fusion.1), channel_id=1, replica_groups=mesh['facet'=8,'slab'=4] {'slab'}, dimensions={1}, use_global_device_ids=true | all-gather | bytes 327680 | tf_op jit(solution)/shard_map/all_gather | solution.py:181
  87.7 0.0 all-gather.2.cloned.1.call-update
  87.7 0.7 fusion.3
  88.4 26.4 %all-gather.2.cloned.1.call-done.sent_ref = bf16[2,4,8,64,256]{4,3,2,1,0:T(8,128)(2,1)} async-done(((bf16[2,4,1,64,256]{4,3,2,1,0:T(8,128)(2,1)}), bf16[2,4,8,64,256]{4,3,2,1,0:T(8,128)(2,1)}) %all-gather.2.cloned.1.call-update) | async-done | bytes 2097168 | tf_op jit(solution)/shard_map/all_gather | solution.py:182
  114.8 9.7 %adjoint.1 = f32[2,1024,256]{2,1,0:T(8,128)} custom-call(s32[1]{0:T(128)S(6)} %add.7.first_ref, s32[1,8]{1,0:T(1,128)} %bitcast.32, bf16[2,4,8,64,256]{4,3,2,1,0:T(8,128)(2,1)} %all-gather.2.cloned.1.call-done.sent_ref), custom_call_target="tpu_custom_call" | custom-call | tf_op jit(solution)/shard_map/adjoint/pallas_call | solution.py:148
  (2 shorter events, 0.1 us)
Async XLA Ops:
  21.0 5.3 %copy-start = (f32[2,1,1,32768]{3,2,1,0:T(1,128)S(1)}, f32[2,1,1,32768]{3,2,1,0:T(1,128)}, u32[]{:S(2)}) copy-start(f32[2,1,1,32768]{3,2,1,0:T(1,128)} %param.10) | copy-start | bytes 786436
  21.0 31.9 %all-to-all-start = ((bf16[2,4,8,64,256]{4,3,1,0,2:T(8,128)(2,1)}), bf16[2,4,8,64,256]{4,3,1,0,2:T(8,128)(2,1)S(1)}, u32[]{:S(2)}, u32[]{:S(2)}) async-start(bf16[2,4,8,64,256]{4,3,1,0,2:T(8,128)(2,1)} %copy.13), calls=%async_computation | async-start | bytes 4194304 | tf_op jit(solution)/shard_map/all_to_all | solution.py:174
  54.1 17.8 %all-to-all-start.1 = ((bf16[2,4,64,256]{3,2,0,1:T(8,128)(2,1)}), bf16[2,4,64,256]{3,2,0,1:T(8,128)(2,1)S(1)}, u32[]{:S(2)}, u32[]{:S(2)}) async-start(bf16[2,4,64,256]{3,2,0,1:T(8,128)(2,1)} %copy.14), calls=%async_computation.1 | async-start | bytes 524288 | tf_op jit(solution)/shard_map/all_to_all | solution.py:176
  58.9 55.8 %all-gather.2.cloned.1.call-start = ((), (), s32[]{:S(2)}) async-start(), calls=%async_computation.2 | async-start | bytes 2359296 | tf_op jit(solution)/shard_map/all_gather | solution.py:182
Sparse Core Ops, SparseCore 0:
  87.8 26.9 all-gather.1

commit v2 on v1

--- a/solution.py
+++ b/solution.py
@@ -159,6 +159,261 @@
     )(first, subs[None, :], sent)
 
 
+def fused_kernel(
+    scale, back, subs_ref, subv_ref, places_ref, ycol_ref, slab_ref, cell_ref, value_ref, weight_ref,
+    residual_ref, update_ref,
+    pslab, pplaces, cos_ref, sin_ref, acc, cb, rx, zf, zb, rz, sums, full, table,
+    sw_send, sw_recv, x_send, x_recv, z_send, z_recv, gz_send, gz_recv, gx_send, gx_recv, gc_send, gc_recv,
+):
+    facets, slabs = lax.axis_size("facet"), lax.axis_size("slab")
+    q, z = lax.axis_index("facet"), lax.axis_index("slab")
+    core, chip = q % 2, q // 2
+    chips = facets // 2
+    partner = q + 1 - 2 * core
+    _, local, width = slab_ref.shape
+    band = SG // slabs
+    dot = functools.partial(jnp.dot, preferred_element_type=F32)
+
+    def at_chip(d):
+        return 2 * ((chip + d) % chips) + core
+
+    def from_chip(d):
+        return 2 * ((chip + chips - d) % chips) + core
+
+    def at_slab(e):
+        return (z + e) % slabs
+
+    def from_slab(e):
+        return (z + slabs - e) % slabs
+
+    def remote(src, dst, send, recv, **where):
+        return pltpu.make_async_remote_copy(
+            src_ref=src, dst_ref=dst, send_sem=send, recv_sem=recv,
+            device_id=where, device_id_type=pl.DeviceIdType.MESH,
+        )
+
+    barrier = pltpu.get_barrier_semaphore()
+    pl.semaphore_signal(barrier, inc=1, device_id={"facet": partner}, device_id_type=pl.DeviceIdType.MESH)
+    for d in range(1, chips):
+        pl.semaphore_signal(barrier, inc=1, device_id={"facet": at_chip(d)}, device_id_type=pl.DeviceIdType.MESH)
+    for e in range(1, slabs):
+        pl.semaphore_signal(barrier, inc=1, device_id={"slab": at_slab(e)}, device_id_type=pl.DeviceIdType.MESH)
+    pl.semaphore_wait(barrier, chips + slabs - 1)
+
+    swap_places = remote(places_ref, pplaces, sw_send.at[0], sw_recv.at[0], facet=partner)
+    swap_slab = remote(slab_ref, pslab, sw_send.at[1], sw_recv.at[1], facet=partner)
+    swap_places.start()
+    swap_slab.start()
+
+    def build(y_ref, slot):
+        def step(i, carry):
+            k = lax.broadcasted_iota(jnp.int32, (32, local), 0) + i * 32
+            c, n = cis((UVSTEP * k) * y_ref[0:1, :])
+            at = pl.ds(pl.multiple_of(i * 32, 32), 32)
+            cos_ref[slot, at] = c
+            sin_ref[slot, at] = n
+            return carry
+
+        lax.fori_loop(0, SG // 32, step, 0)
+
+    def partial_sum(s, y_ref, slot, data_ref):
+        c1, s1 = cis(subs_ref[s] * y_ref[...])
+        c1, s1 = c1[0:1], s1[0:1]
+        c2, s2 = cos_ref[slot], sin_ref[slot]
+        tab_real = (c1 * c2 - s1 * s2).astype(BF16)
+        tab_imag = (-(s1 * c2 + c1 * s2)).astype(BF16)
+        re, im = data_ref[0], data_ref[1]
+        return dot(tab_real, re) - dot(tab_imag, im), dot(tab_real, im) + dot(tab_imag, re)
+
+    build(places_ref, 0)
+
+    def own_part(d, carry):
+        real, imag = partial_sum(at_chip(d), places_ref, 0, slab_ref)
+        acc[d, 0] = real
+        acc[d, 1] = imag
+        return carry
+
+    lax.fori_loop(0, chips, own_part, 0)
+    swap_places.wait()
+    build(pplaces, 1)
+    swap_slab.wait()
+    x_copies = []
+    for d in list(range(1, chips)) + [0]:
+        real, imag = partial_sum(at_chip(d), pplaces, 1, pslab)
+        if d == 0:
+            acc[0, 0] += real
+            acc[0, 1] += imag
+        else:
+            cb[d - 1, 0] = (acc[d, 0] + real).astype(BF16)
+            cb[d - 1, 1] = (acc[d, 1] + imag).astype(BF16)
+            copy = remote(cb.at[d - 1], rx.at[d - 1], x_send.at[d - 1], x_recv.at[d - 1], facet=at_chip(d))
+            copy.start()
+            x_copies.append(copy)
+
+    rows = sums.shape[0] // 3
+    count = cell_ref.shape[1]
+    chunk = min(count, 2048)
+    sums[...] = jnp.zeros_like(sums)
+
+    def grid_step(i, carry):
+        at = pl.ds(pl.multiple_of(i * chunk, chunk), chunk)
+        cell = cell_ref[:, at]
+        weight = weight_ref[:, at]
+        row = lax.shift_right_logical(cell, width.bit_length() - 1)
+        col = cell & (width - 1)
+        hot = jnp.where(lax.broadcasted_iota(jnp.int32, (width, chunk), 0) == col, 1.0, 0.0).astype(BF16)
+        mine = lax.broadcasted_iota(jnp.int32, (rows, chunk), 0) == row
+        terms = [weight * value_ref[0:1, at], weight * value_ref[1:2, at], weight]
+        left = jnp.concatenate([jnp.where(mine, t, 0.0).astype(BF16) for t in terms], axis=0)
+        sums[...] += lax.dot_general(left, hot, (((1,), (1,)), ((), ())), preferred_element_type=F32)
+        return carry
+
+    lax.fori_loop(0, count // chunk, grid_step, 0)
+
+    for copy in x_copies:
+        copy.wait()
+    for p in range(slabs):
+        for c in range(2):
+            at = slice(p * band, (p + 1) * band)
+            total = acc[0, c, at]
+            for d in range(1, chips):
+                total += rx[d - 1, c, at].astype(F32)
+            zf[p, c] = total
+            zb[p, c] = total.astype(BF16)
+    z_copies = []
+    for e in range(1, slabs):
+        copy = remote(zb.at[at_slab(e)], rz.at[e - 1], z_send.at[e - 1], z_recv.at[e - 1], slab=at_slab(e))
+        copy.start()
+        z_copies.append(copy)
+
+    tile = min(local, 256)
+
+    def table_step(i, carry):
+        at = pl.ds(pl.multiple_of(i * tile, tile), tile)
+        y = ycol_ref[at, 0:1]
+        c2, s2 = cis((UVSTEP * lax.broadcasted_iota(jnp.int32, (tile, SG), 1)) * y)
+        c1, s1 = cis(y * subv_ref[...])
+        for s in range(facets):
+            a, b = c1[:, s:s + 1], s1[:, s:s + 1]
+            table[s, 0, at] = (a * c2 - b * s2).astype(BF16)
+            table[s, 1, at] = (-(b * c2 + a * s2)).astype(BF16)
+        return carry
+
+    lax.fori_loop(0, local // tile, table_step, 0)
+
+    for copy in z_copies:
+        copy.wait()
+    for c in range(2):
+        model = zf[z, c]
+        for e in range(1, slabs):
+            model += rz[e - 1, c].astype(F32)
+        piece = sums[c * rows:c * rows + band] - sums[2 * rows:2 * rows + band] * (model * scale)
+        residual_ref[c] = piece
+        full[q, z, c] = piece.astype(BF16)
+
+    late = []
+
+    def spread(s, p, e, d):
+        ref = full.at[s, p]
+        copy = remote(ref, ref, gc_send.at[e, d], gc_recv.at[e, d], facet=partner)
+        copy.start()
+        late.append(copy)
+
+    def across(p, e):
+        ref = full.at[q, p]
+        out = []
+        for d in range(1, chips):
+            copy = remote(ref, ref, gx_send.at[e, d - 1], gx_recv.at[e, d - 1], facet=at_chip(d))
+            copy.start()
+            out.append(copy)
+        return out
+
+    own = full.at[q, z]
+    g_copies = []
+    for e in range(1, slabs):
+        copy = remote(own, own, gz_send.at[e - 1], gz_recv.at[e - 1], slab=at_slab(e))
+        copy.start()
+        g_copies.append(copy)
+    a_copies = [across(z, 0)]
+    spread(q, z, 0, 0)
+    for e in range(1, slabs):
+        g_copies[e - 1].wait_recv()
+        a_copies.append(across(from_slab(e), e))
+        spread(q, from_slab(e), e, 0)
+    for e in range(slabs):
+        for d in range(1, chips):
+            a_copies[e][d - 1].wait_recv()
+            spread(from_chip(d), from_slab(e), e, d)
+    for copy in g_copies:
+        copy.wait_send()
+    for row in a_copies:
+        for copy in row:
+            copy.wait_send()
+    for copy in late:
+        copy.wait()
+
+    def update_step(i, carry):
+        at = pl.ds(pl.multiple_of(i * tile, tile), tile)
+        real = jnp.zeros((tile, width), F32)
+        imag = jnp.zeros((tile, width), F32)
+        for s in range(facets):
+            tab_real, tab_imag = table[s, 0, at], table[s, 1, at]
+            re = jnp.concatenate([full[s, p, 0] for p in range(slabs)], axis=0)
+            im = jnp.concatenate([full[s, p, 1] for p in range(slabs)], axis=0)
+            real += dot(tab_real, re) + dot(tab_imag, im)
+            imag += dot(tab_real, im) - dot(tab_imag, re)
+        update_ref[0, at] = real * back
+        update_ref[1, at] = imag * back
+        return carry
+
+    lax.fori_loop(0, local // tile, update_step, 0)
+
+
+def fused(first, subs, slab, cells, values, weights, slabs, facets):
+    _, local, width = slab.shape
+    band = SG // slabs
+    chips = facets // 2
+    rows = -(-band // 16) * 16
+    places = first + lax.broadcasted_iota(jnp.int32, (8, local), 1)
+    ycol = first + lax.broadcasted_iota(jnp.int32, (local, 8), 0)
+    vmem = pl.BlockSpec(memory_space=pltpu.VMEM)
+    dma = pltpu.SemaphoreType.DMA
+    return pl.pallas_call(
+        functools.partial(
+            fused_kernel, 1.0 / math.sqrt(local * slabs * facets), 1.0 / math.sqrt(subs.shape[0] * SG)
+        ),
+        in_specs=[pl.BlockSpec(memory_space=pltpu.SMEM)] + [vmem] * 7,
+        out_specs=[vmem, vmem],
+        out_shape=[
+            jax.ShapeDtypeStruct((2, band, width), F32),
+            jax.ShapeDtypeStruct((2, local, width), F32),
+        ],
+        scratch_shapes=[
+            pltpu.VMEM((2, local, width), BF16),
+            pltpu.VMEM((8, local), jnp.int32),
+            pltpu.VMEM((2, SG, local), F32),
+            pltpu.VMEM((2, SG, local), F32),
+            pltpu.VMEM((chips, 2, SG, width), F32),
+            pltpu.VMEM((chips - 1, 2, SG, width), BF16),
+            pltpu.VMEM((chips - 1, 2, SG, width), BF16),
+            pltpu.VMEM((slabs, 2, band, width), F32),
+            pltpu.VMEM((slabs, 2, band, width), BF16),
+            pltpu.VMEM((slabs - 1, 2, band, width), BF16),
+            pltpu.VMEM((3 * rows, width), F32),
+            pltpu.VMEM((facets, slabs, 2, band, width), BF16),
+            pltpu.VMEM((facets, 2, local, SG), BF16),
+            dma((2,)), dma((2,)),
+            dma((chips - 1,)), dma((chips - 1,)),
+            dma((slabs - 1,)), dma((slabs - 1,)),
+            dma((slabs - 1,)), dma((slabs - 1,)),
+            dma((slabs, chips - 1)), dma((slabs, chips - 1)),
+            dma((slabs, chips)), dma((slabs, chips)),
+        ],
+        compiler_params=pltpu.CompilerParams(collective_id=0, has_side_effects=True, vmem_limit_bytes=60 * 1024 * 1024),
+        name="fused",
+    )(subs, subs[None, :], places, ycol, slab, cells, values, weights)
+
+
 def body(slab, facet_offset, subgrid_offset, vis_cell, vis_value, vis_weight):
     slabs = lax.axis_size("slab")
     facets = lax.axis_size("facet")
@@ -168,6 +423,11 @@
     band = SG // slabs
     owned = count_sub * band // facets
     first = (facet_offset + lax.axis_index("slab") * local_rows).astype(jnp.int32)
+    if owned == band and facets % 2 == 0 and facets > 2 and slabs > 1 and band % 16 == 0:
+        residual, update = fused(
+            first, subgrid_offset, slab[:, 0], vis_cell[0], vis_value[:, 0, 0], vis_weight[0], slabs, facets
+        )
+        return (residual.reshape(2, 1, owned, width), update.reshape(2, 1, local_rows, width))
     sums = grid_visibilities(vis_cell[0], vis_value[:, 0, 0], vis_weight[0], owned, width)
     contrib = forward(first, subgrid_offset, slab[:, 0], slabs)
     contrib = contrib.reshape(2, slabs, facets, owned, width)

time: 132 us -> 65.3 us (0.49)
  the two profiles are of different devices: /device:TPU:0 before, /device:TPU:23 now
where the time goes in v2:
time: 65.3 us; the launch traced here: 65.1 us
  Pallas kernels  55.7 us (85%)
  local copies, waits for them, and re-layouts  8.12 us (12%)
  between operations  1.3 us (2%)
    pallas_call x1, Pallas kernels, fused(): pl.pallas_call(functools.partial(fused_kernel, 1.0 / math.sqrt(local * sl...  55.7 us
    unnamed x3, local copies, waits for them, and re-layouts  6.5 us

profile of v2, /device:TPU:23, one launch (start us, length us, event | category | flops | bytes accessed | tf_op | source)
XLA Modules:
  0.0 65.1 jit_solution(5600939481518855977)
XLA Ops:
  1.3 0.6 iota.11.places_ref
  1.9 1.9 %copy.12 = f32[2,1,1,32768]{3,0,1,2:T(2,128)} copy(f32[2,1,1,32768]{3,2,1,0:T(1,128)} %param.10) | data formatting | bytes 524288
  3.8 1.0 %iota.12.ycol_ref = s32[1024,8]{1,0:T(8,128)} broadcast(s32[1024]{0:T(1024)S(1)} %iota_add_fusion), dimensions={0} | broadcast | bytes 36864 | tf_op jit(solution)/shard_map/iota | solution.py:378
  4.8 55.7 %fused.1 = (f32[2,64,256]{2,1,0:T(8,128)}, f32[2,1024,256]{2,1,0:T(8,128)}) custom-call(s32[8]{0:T(128)} %subs_ref.1, s32[1,8]{1,0:T(1,128)} %bitcast.21, s32[8,1024]{1,0:T(8,128)} %iota.11.places_ref, s32[1024,8]{1,0:T(8,128)} %iota.12.ycol_ref, bf16[2,1024,256]{2,1,0:T(8,128)(2,1)} %bitcast.16, s32[1,32768]{1,0:T(1,128)} %bitcast.19, f32[2,32768]{1,0:T(2,128)} %bitcast.17, ...), custom_call_target="tpu_custom_call" | custom-call | tf_op jit(solution)/shard_map/fused/pallas_call | solution.py:381
  60.5 1.6 %copy.16 = f32[2,1,64,256]{3,2,1,0:T(8,128)} copy(f32[2,1,64,256]{3,2,1,0:T(8,128)} %bitcast.18) | data formatting | bytes 262144
  62.0 3.0 %copy.17 = f32[2,1,1024,256]{3,2,1,0:T(8,128)} copy(f32[2,1,1024,256]{3,2,1,0:T(8,128)} %bitcast.15) | data formatting | bytes 4194304
  (1 shorter events, 0.0 us)

commit v3 on v2

--- a/solution.py
+++ b/solution.py
@@ -160,9 +160,9 @@
 
 
 def fused_kernel(
-    scale, back, subs_ref, subv_ref, places_ref, ycol_ref, slab_ref, cell_ref, value_ref, weight_ref,
+    scale, back, subs_ref, offset_ref, subv_ref, offv_ref, slab_ref, cell_ref, value_ref, weight_ref,
     residual_ref, update_ref,
-    pslab, pplaces, cos_ref, sin_ref, acc, cb, rx, zf, zb, rz, sums, full, table,
+    pslab, poff, cos_ref, sin_ref, acc, cb, rx, zf, zb, rz, sums, full, table,
     sw_send, sw_recv, x_send, x_recv, z_send, z_recv, gz_send, gz_recv, gx_send, gx_recv, gc_send, gc_recv,
 ):
     facets, slabs = lax.axis_size("facet"), lax.axis_size("slab")
@@ -200,15 +200,17 @@
         pl.semaphore_signal(barrier, inc=1, device_id={"slab": at_slab(e)}, device_id_type=pl.DeviceIdType.MESH)
     pl.semaphore_wait(barrier, chips + slabs - 1)
 
-    swap_places = remote(places_ref, pplaces, sw_send.at[0], sw_recv.at[0], facet=partner)
+    swap_offset = remote(offv_ref, poff, sw_send.at[0], sw_recv.at[0], facet=partner)
     swap_slab = remote(slab_ref, pslab, sw_send.at[1], sw_recv.at[1], facet=partner)
-    swap_places.start()
+    swap_offset.start()
     swap_slab.start()
 
-    def build(y_ref, slot):
+    first = offset_ref[0] + z * local
+
+    def build(y, slot):
         def step(i, carry):
             k = lax.broadcasted_iota(jnp.int32, (32, local), 0) + i * 32
-            c, n = cis((UVSTEP * k) * y_ref[0:1, :])
+            c, n = cis((UVSTEP * k) * y[0:1, :])
             at = pl.ds(pl.multiple_of(i * 32, 32), 32)
             cos_ref[slot, at] = c
             sin_ref[slot, at] = n
@@ -216,8 +218,8 @@
 
         lax.fori_loop(0, SG // 32, step, 0)
 
-    def partial_sum(s, y_ref, slot, data_ref):
-        c1, s1 = cis(subs_ref[s] * y_ref[...])
+    def partial_sum(s, y, slot, data_ref):
+        c1, s1 = cis(subs_ref[s] * y)
         c1, s1 = c1[0:1], s1[0:1]
         c2, s2 = cos_ref[slot], sin_ref[slot]
         tab_real = (c1 * c2 - s1 * s2).astype(BF16)
@@ -225,16 +227,19 @@
         re, im = data_ref[0], data_ref[1]
         return dot(tab_real, re) - dot(tab_imag, im), dot(tab_real, im) + dot(tab_imag, re)
 
-    build(places_ref, 0)
+    line = lax.broadcasted_iota(jnp.int32, (8, local), 1)
+    places = line + first
+    build(places, 0)
 
     def own_part(d, carry):
-        real, imag = partial_sum(at_chip(d), places_ref, 0, slab_ref)
+        real, imag = partial_sum(at_chip(d), places, 0, slab_ref)
         acc[d, 0] = real
         acc[d, 1] = imag
         return carry
 
     lax.fori_loop(0, chips, own_part, 0)
-    swap_places.wait()
+    swap_offset.wait()
+    pplaces = line + (poff[:, 0:1] + z * local)
     build(pplaces, 1)
     swap_slab.wait()
     x_copies = []
@@ -259,16 +264,27 @@
         at = pl.ds(pl.multiple_of(i * chunk, chunk), chunk)
         cell = cell_ref[:, at]
         weight = weight_ref[:, at]
-        row = lax.shift_right_logical(cell, width.bit_length() - 1)
-        col = cell & (width - 1)
-        hot = jnp.where(lax.broadcasted_iota(jnp.int32, (width, chunk), 0) == col, 1.0, 0.0).astype(BF16)
-        mine = lax.broadcasted_iota(jnp.int32, (rows, chunk), 0) == row
-        terms = [weight * value_ref[0:1, at], weight * value_ref[1:2, at], weight]
-        left = jnp.concatenate([jnp.where(mine, t, 0.0).astype(BF16) for t in terms], axis=0)
+        row = lax.shift_right_logical(cell, width.bit_length() - 1).astype(F32)
+        col = (cell & (width - 1)).astype(F32)
+        lines = lax.broadcasted_iota(jnp.int32, (16, chunk), 0).astype(F32).astype(BF16)
+        row = jnp.broadcast_to(row, (16, chunk)).astype(BF16)
+        col = jnp.broadcast_to(col, (16, chunk)).astype(BF16)
+        one, zero = jnp.ones((16, chunk), BF16), jnp.zeros((16, chunk), BF16)
+        hot = jnp.concatenate(
+            [jnp.where(col == lines + jnp.asarray(g, BF16), one, zero) for g in range(0, width, 16)], axis=0
+        )
+        terms = [weight * value_ref[0, :, at], weight * value_ref[1, :, at], weight]
+        terms = [jnp.broadcast_to(t, (16, chunk)).astype(BF16) for t in terms]
+        left = jnp.concatenate(
+            [jnp.where(row == lines + jnp.asarray(g, BF16), t, zero) for t in terms for g in range(0, rows, 16)],
+            axis=0,
+        )
         sums[...] += lax.dot_general(left, hot, (((1,), (1,)), ((), ())), preferred_element_type=F32)
         return carry
 
-    lax.fori_loop(0, count // chunk, grid_step, 0)
+    chunks = count // chunk
+    early = (5 * chunks) // 8
+    lax.fori_loop(0, early, grid_step, 0)
 
     for copy in x_copies:
         copy.wait()
@@ -288,18 +304,7 @@
 
     tile = min(local, 256)
 
-    def table_step(i, carry):
-        at = pl.ds(pl.multiple_of(i * tile, tile), tile)
-        y = ycol_ref[at, 0:1]
-        c2, s2 = cis((UVSTEP * lax.broadcasted_iota(jnp.int32, (tile, SG), 1)) * y)
-        c1, s1 = cis(y * subv_ref[...])
-        for s in range(facets):
-            a, b = c1[:, s:s + 1], s1[:, s:s + 1]
-            table[s, 0, at] = (a * c2 - b * s2).astype(BF16)
-            table[s, 1, at] = (-(b * c2 + a * s2)).astype(BF16)
-        return carry
-
-    lax.fori_loop(0, local // tile, table_step, 0)
+    lax.fori_loop(early, chunks, grid_step, 0)
 
     for copy in z_copies:
         copy.wait()
@@ -311,6 +316,17 @@
         residual_ref[c] = piece
         full[q, z, c] = piece.astype(BF16)
 
+    def table_step(i, carry):
+        at = pl.ds(pl.multiple_of(i * tile, tile), tile)
+        y = lax.broadcasted_iota(jnp.int32, (tile, 1), 0) + (first + i * tile)
+        c2, s2 = cis((UVSTEP * lax.broadcasted_iota(jnp.int32, (tile, SG), 1)) * y)
+        c1, s1 = cis(y * subv_ref[...])
+        for s in range(facets):
+            a, b = c1[:, s:s + 1], s1[:, s:s + 1]
+            table[s, 0, at] = (a * c2 - b * s2).astype(BF16)
+            table[s, 1, at] = (-(b * c2 + a * s2)).astype(BF16)
+        return carry
+
     late = []
 
     def spread(s, p, e, d):
@@ -336,53 +352,74 @@
         g_copies.append(copy)
     a_copies = [across(z, 0)]
     spread(q, z, 0, 0)
+    tiles = local // tile
+    done = 0
     for e in range(1, slabs):
+        share = (e * tiles) // slabs
+        lax.fori_loop(done, share, table_step, 0)
+        done = share
         g_copies[e - 1].wait_recv()
         a_copies.append(across(from_slab(e), e))
         spread(q, from_slab(e), e, 0)
-    for e in range(slabs):
+    lax.fori_loop(done, tiles, table_step, 0)
+
+    def update_pass(which, begin, end):
+        def step(i, carry):
+            at = pl.ds(pl.multiple_of(i * tile, tile), tile)
+            real = imag = None
+            for s in which:
+                tab_real, tab_imag = table[s, 0, at], table[s, 1, at]
+                re = jnp.concatenate([full[s, p, 0] for p in range(slabs)], axis=0)
+                im = jnp.concatenate([full[s, p, 1] for p in range(slabs)], axis=0)
+                dr = dot(tab_real, re) + dot(tab_imag, im)
+                di = dot(tab_real, im) - dot(tab_imag, re)
+                real = dr if real is None else real + dr
+                imag = di if imag is None else imag + di
+            if not begin:
+                real += update_ref[0, at]
+                imag += update_ref[1, at]
+            update_ref[0, at] = real * back if end else real
+            update_ref[1, at] = imag * back if end else imag
+            return carry
+
+        lax.fori_loop(0, tiles, step, 0)
+
+    def relay(e):
         for d in range(1, chips):
             a_copies[e][d - 1].wait_recv()
             spread(from_chip(d), from_slab(e), e, d)
-    for copy in g_copies:
+
+    relay(0)
+    update_pass([q], True, False)
+    for e in range(1, slabs - 1):
+        relay(e)
+    for copy in late[:slabs]:
+        copy.wait_recv()
+    update_pass([partner], False, False)
+    relay(slabs - 1)
+    update_pass([from_chip(d) for d in range(1, chips)], False, False)
+    for copy in late[slabs:]:
+        copy.wait_recv()
+    update_pass([from_chip(d) + 1 - 2 * core for d in range(1, chips)], False, True)
+    for copy in g_copies + late:
         copy.wait_send()
-    for row in a_copies:
-        for copy in row:
+    for group in a_copies:
+        for copy in group:
             copy.wait_send()
-    for copy in late:
-        copy.wait()
-
-    def update_step(i, carry):
-        at = pl.ds(pl.multiple_of(i * tile, tile), tile)
-        real = jnp.zeros((tile, width), F32)
-        imag = jnp.zeros((tile, width), F32)
-        for s in range(facets):
-            tab_real, tab_imag = table[s, 0, at], table[s, 1, at]
-            re = jnp.concatenate([full[s, p, 0] for p in range(slabs)], axis=0)
-            im = jnp.concatenate([full[s, p, 1] for p in range(slabs)], axis=0)
-            real += dot(tab_real, re) + dot(tab_imag, im)
-            imag += dot(tab_real, im) - dot(tab_imag, re)
-        update_ref[0, at] = real * back
-        update_ref[1, at] = imag * back
-        return carry
-
-    lax.fori_loop(0, local // tile, update_step, 0)
-
-
-def fused(first, subs, slab, cells, values, weights, slabs, facets):
+
+
+def fused(offset, subs, slab, cells, values, weights, slabs, facets):
     _, local, width = slab.shape
     band = SG // slabs
     chips = facets // 2
     rows = -(-band // 16) * 16
-    places = first + lax.broadcasted_iota(jnp.int32, (8, local), 1)
-    ycol = first + lax.broadcasted_iota(jnp.int32, (local, 8), 0)
     vmem = pl.BlockSpec(memory_space=pltpu.VMEM)
     dma = pltpu.SemaphoreType.DMA
     return pl.pallas_call(
         functools.partial(
             fused_kernel, 1.0 / math.sqrt(local * slabs * facets), 1.0 / math.sqrt(subs.shape[0] * SG)
         ),
-        in_specs=[pl.BlockSpec(memory_space=pltpu.SMEM)] + [vmem] * 7,
+        in_specs=[pl.BlockSpec(memory_space=pltpu.SMEM)] * 2 + [vmem] * 6,
         out_specs=[vmem, vmem],
         out_shape=[
             jax.ShapeDtypeStruct((2, band, width), F32),
@@ -390,7 +427,7 @@
         ],
         scratch_shapes=[
             pltpu.VMEM((2, local, width), BF16),
-            pltpu.VMEM((8, local), jnp.int32),
+            pltpu.VMEM((8, 128), jnp.int32),
             pltpu.VMEM((2, SG, local), F32),
             pltpu.VMEM((2, SG, local), F32),
             pltpu.VMEM((chips, 2, SG, width), F32),
@@ -409,9 +446,9 @@
             dma((slabs, chips - 1)), dma((slabs, chips - 1)),
             dma((slabs, chips)), dma((slabs, chips)),
         ],
-        compiler_params=pltpu.CompilerParams(collective_id=0, has_side_effects=True, vmem_limit_bytes=60 * 1024 * 1024),
+        compiler_params=pltpu.CompilerParams(collective_id=0, has_side_effects=True, vmem_limit_bytes=36 * 1024 * 1024),
         name="fused",
-    )(subs, subs[None, :], places, ycol, slab, cells, values, weights)
+    )(subs, offset, subs[None, :], jnp.broadcast_to(offset, (8, 128)), slab, cells, values, weights)
 
 
 def body(slab, facet_offset, subgrid_offset, vis_cell, vis_value, vis_weight):
@@ -425,7 +462,7 @@
     first = (facet_offset + lax.axis_index("slab") * local_rows).astype(jnp.int32)
     if owned == band and facets % 2 == 0 and facets > 2 and slabs > 1 and band % 16 == 0:
         residual, update = fused(
-            first, subgrid_offset, slab[:, 0], vis_cell[0], vis_value[:, 0, 0], vis_weight[0], slabs, facets
+            facet_offset, subgrid_offset, slab[:, 0], vis_cell[0], vis_value[:, 0], vis_weight[0], slabs, facets
         )
         return (residual.reshape(2, 1, owned, width), update.reshape(2, 1, local_rows, width))
     sums = grid_visibilities(vis_cell[0], vis_value[:, 0, 0], vis_weight[0], owned, width)

time: 65.3 us -> 59.6 us (0.913)
  the two profiles are of different devices: /device:TPU:23 before, /device:TPU:0 now
where the time goes in v3:
time: 59.6 us; the launch traced here: 58.6 us
  Pallas kernels  50.6 us (85%)
  local copies, waits for them, and re-layouts  6.61 us (11%)
  between operations  1.31 us (2%)
    pallas_call x1, Pallas kernels, fused(): pl.pallas_call(functools.partial(fused_kernel, 1.0 / math.sqrt(local * sl...  50.6 us
    unnamed x12, local copies, waits for them, and re-layouts  6.61 us

profile of v3, /device:TPU:0, one launch (start us, length us, event | category | flops | bytes accessed | tf_op | source)
XLA Modules:
  0.0 58.6 jit_solution(11413973841380541350)
XLA Ops:
  1.3 0.0 copy-start
  1.3 1.2 %copy-done = bf16[2,1,1024,256]{3,2,1,0:T(8,128)(2,1)S(1)} copy-done((bf16[2,1,1024,256]{3,2,1,0:T(8,128)(2,1)S(1)}, bf16[2,1,1024,256]{3,2,1,0:T(8,128)(2,1)}, u32[]{:S(2)}) %copy-start) | copy-done | bytes 1048600
  2.5 0.0 copy-start.1
  2.5 0.9 %copy-done.1 = f32[2,1,1,32768]{3,2,1,0:T(1,128)S(1)} copy-done((f32[2,1,1,32768]{3,2,1,0:T(1,128)S(1)}, f32[2,1,1,32768]{3,2,1,0:T(1,128)}, u32[]{:S(2)}) %copy-start.1) | copy-done | bytes 262168
  3.5 0.0 copy-start.2
  3.5 0.9 %copy-done.2 = s32[1,1,32768]{2,1,0:T(1,128)S(1)} copy-done((s32[1,1,32768]{2,1,0:T(1,128)S(1)}, s32[1,1,32768]{2,1,0:T(1,128)}, u32[]{:S(2)}) %copy-start.2) | copy-done | bytes 131096
  4.4 0.0 copy-start.3
  4.4 0.9 %copy-done.3 = f32[1,1,32768]{2,1,0:T(1,128)S(1)} copy-done((f32[1,1,32768]{2,1,0:T(1,128)S(1)}, f32[1,1,32768]{2,1,0:T(1,128)}, u32[]{:S(2)}) %copy-start.3) | copy-done | bytes 131096
  5.3 0.0 copy-start.4
  5.3 0.7 %copy-done.4 = s32[8]{0:T(128)S(1)} copy-done((s32[8]{0:T(128)S(1)}, s32[8]{0:T(128)}, u32[]{:S(2)}) %copy-start.4) | copy-done | bytes 56
  5.9 50.6 %fused.1 = (f32[2,64,256]{2,1,0:T(8,128)S(1)}, f32[2,1024,256]{2,1,0:T(8,128)S(1)}) custom-call(s32[8]{0:T(128)S(1)} %copy-done.4, s32[1]{0:T(128)} %copy.12.offset_ref, s32[1,8]{1,0:T(1,128)S(1)} %bitcast.19, s32[8,128]{1,0:T(8,128)S(1)} %broadcast_in_dim.9.offv_ref, bf16[2,1024,256]{2,1,0:T(8,128)(2,1)S(1)} %bitcast.14, s32[1,32768]{1,0:T(1,128)S(1)} %bitcast.16, ...), custom_call_target="tpu_custom_call" | custom-call | tf_op jit(solution)/shard_map/fused/pallas_call | solution.py:418
  56.6 0.7 %copy.13 = f32[2,1,64,256]{3,2,1,0:T(8,128)} copy(f32[2,1,64,256]{3,2,1,0:T(8,128)S(1)} %bitcast.18) | data formatting | bytes 262144
  57.2 1.3 %copy.14 = f32[2,1,1024,256]{3,2,1,0:T(8,128)} copy(f32[2,1,1024,256]{3,2,1,0:T(8,128)S(1)} %bitcast.13) | data formatting | bytes 4194304
  (1 shorter events, 0.0 us)
Async XLA Ops:
  1.3 1.2 %copy-start = (bf16[2,1,1024,256]{3,2,1,0:T(8,128)(2,1)S(1)}, bf16[2,1,1024,256]{3,2,1,0:T(8,128)(2,1)}, u32[]{:S(2)}) copy-start(bf16[2,1,1024,256]{3,2,1,0:T(8,128)(2,1)} %param.6) | copy-start | bytes 3145732
  2.5 0.9 %copy-start.1 = (f32[2,1,1,32768]{3,2,1,0:T(1,128)S(1)}, f32[2,1,1,32768]{3,2,1,0:T(1,128)}, u32[]{:S(2)}) copy-start(f32[2,1,1,32768]{3,2,1,0:T(1,128)} %param.10) | copy-start | bytes 786436
  3.5 0.9 %copy-start.2 = (s32[1,1,32768]{2,1,0:T(1,128)S(1)}, s32[1,1,32768]{2,1,0:T(1,128)}, u32[]{:S(2)}) copy-start(s32[1,1,32768]{2,1,0:T(1,128)} %param.9) | copy-start | bytes 393220
  4.4 0.9 %copy-start.3 = (f32[1,1,32768]{2,1,0:T(1,128)S(1)}, f32[1,1,32768]{2,1,0:T(1,128)}, u32[]{:S(2)}) copy-start(f32[1,1,32768]{2,1,0:T(1,128)} %param.11) | copy-start | bytes 393220
  5.3 0.7 %copy-start.4 = (s32[8]{0:T(128)S(1)}, s32[8]{0:T(128)}, u32[]{:S(2)}) copy-start(s32[8]{0:T(128)} %subs_ref.1) | copy-start | bytes 100

commit v4 on v3

--- a/solution.py
+++ b/solution.py
@@ -160,9 +160,9 @@
 
 
 def fused_kernel(
-    scale, back, subs_ref, offset_ref, subv_ref, offv_ref, slab_ref, cell_ref, value_ref, weight_ref,
+    scale, back, subs_ref, offset_ref, offv_ref, slab_hbm, cell_hbm, value_hbm, weight_hbm,
     residual_ref, update_ref,
-    pslab, poff, cos_ref, sin_ref, acc, cb, rx, zf, zb, rz, sums, full, table,
+    slab_ref, cell_ref, value_ref, weight_ref, in_sem, pslab, poff, cos_ref, sin_ref, acc, cb, rx, zf, zb, rz, sums, full, table,
     sw_send, sw_recv, x_send, x_recv, z_send, z_recv, gz_send, gz_recv, gx_send, gx_recv, gc_send, gc_recv,
 ):
     facets, slabs = lax.axis_size("facet"), lax.axis_size("slab")
@@ -170,6 +170,14 @@
     core, chip = q % 2, q // 2
     chips = facets // 2
     partner = q + 1 - 2 * core
+    loads = [
+        pltpu.make_async_copy(src, dst, in_sem.at[n])
+        for n, (src, dst) in enumerate([
+            (slab_hbm, slab_ref), (cell_hbm, cell_ref), (value_hbm, value_ref), (weight_hbm, weight_ref),
+        ])
+    ]
+    for load in loads:
+        load.start()
     _, local, width = slab_ref.shape
     band = SG // slabs
     dot = functools.partial(jnp.dot, preferred_element_type=F32)
@@ -201,7 +209,7 @@
     pl.semaphore_wait(barrier, chips + slabs - 1)
 
     swap_offset = remote(offv_ref, poff, sw_send.at[0], sw_recv.at[0], facet=partner)
-    swap_slab = remote(slab_ref, pslab, sw_send.at[1], sw_recv.at[1], facet=partner)
+    swap_slab = remote(slab_hbm, pslab, sw_send.at[1], sw_recv.at[1], facet=partner)
     swap_offset.start()
     swap_slab.start()
 
@@ -237,6 +245,7 @@
         acc[d, 1] = imag
         return carry
 
+    loads[0].wait()
     lax.fori_loop(0, chips, own_part, 0)
     swap_offset.wait()
     pplaces = line + (poff[:, 0:1] + z * local)
@@ -282,6 +291,8 @@
         sums[...] += lax.dot_general(left, hot, (((1,), (1,)), ((), ())), preferred_element_type=F32)
         return carry
 
+    for load in loads[1:]:
+        load.wait()
     chunks = count // chunk
     early = (5 * chunks) // 8
     lax.fori_loop(0, early, grid_step, 0)
@@ -320,7 +331,11 @@
         at = pl.ds(pl.multiple_of(i * tile, tile), tile)
         y = lax.broadcasted_iota(jnp.int32, (tile, 1), 0) + (first + i * tile)
         c2, s2 = cis((UVSTEP * lax.broadcasted_iota(jnp.int32, (tile, SG), 1)) * y)
-        c1, s1 = cis(y * subv_ref[...])
+        lane = lax.broadcasted_iota(jnp.int32, (1, facets), 1)
+        subs = jnp.zeros((1, facets), jnp.int32)
+        for s in range(facets):
+            subs = jnp.where(lane == s, subs_ref[s], subs)
+        c1, s1 = cis(y * subs)
         for s in range(facets):
             a, b = c1[:, s:s + 1], s1[:, s:s + 1]
             table[s, 0, at] = (a * c2 - b * s2).astype(BF16)
@@ -419,13 +434,18 @@
         functools.partial(
             fused_kernel, 1.0 / math.sqrt(local * slabs * facets), 1.0 / math.sqrt(subs.shape[0] * SG)
         ),
-        in_specs=[pl.BlockSpec(memory_space=pltpu.SMEM)] * 2 + [vmem] * 6,
+        in_specs=[pl.BlockSpec(memory_space=pltpu.SMEM)] * 2 + [vmem] + [pl.BlockSpec(memory_space=pltpu.HBM)] * 4,
         out_specs=[vmem, vmem],
         out_shape=[
             jax.ShapeDtypeStruct((2, band, width), F32),
             jax.ShapeDtypeStruct((2, local, width), F32),
         ],
         scratch_shapes=[
+            pltpu.VMEM(slab.shape, slab.dtype),
+            pltpu.VMEM(cells.shape, cells.dtype),
+            pltpu.VMEM(values.shape, values.dtype),
+            pltpu.VMEM(weights.shape, weights.dtype),
+            dma((4,)),
             pltpu.VMEM((2, local, width), BF16),
             pltpu.VMEM((8, 128), jnp.int32),
             pltpu.VMEM((2, SG, local), F32),
@@ -446,9 +466,9 @@
             dma((slabs, chips - 1)), dma((slabs, chips - 1)),
             dma((slabs, chips)), dma((slabs, chips)),
         ],
-        compiler_params=pltpu.CompilerParams(collective_id=0, has_side_effects=True, vmem_limit_bytes=36 * 1024 * 1024),
+        compiler_params=pltpu.CompilerParams(collective_id=0, has_side_effects=True, vmem_limit_bytes=60 * 1024 * 1024),
         name="fused",
-    )(subs, offset, subs[None, :], jnp.broadcast_to(offset, (8, 128)), slab, cells, values, weights)
+    )(subs, offset, jnp.broadcast_to(offset, (8, 128)), slab, cells, values, weights)
 
 
 def body(slab, facet_offset, subgrid_offset, vis_cell, vis_value, vis_weight):

time: 59.6 us -> 59.7 us (level)
  Pallas kernels: 50.6 us -> 52.1 us
  local copies, waits for them, and re-layouts: 6.61 us -> 5.21 us
    unnamed x12 -> x2, local copies, waits for them, and re-layouts: 6.61 us -> 4.61 us
    pallas_call x1, Pallas kernels: 50.6 us -> 52.1 us  [fused(): pl.pallas_call(functools.partial(fused_kernel, 1.0 / math.sqrt(local * sl...]
where the time goes in v4:
time: 59.7 us; the launch traced here: 58.6 us
  Pallas kernels  52.1 us (87%)
  local copies, waits for them, and re-layouts  5.21 us (9%)
  between operations  1.29 us (2%)
    pallas_call x1, Pallas kernels, fused(): pl.pallas_call(functools.partial(fused_kernel, 1.0 / math.sqrt(local * sl...  52.1 us
    unnamed x2, local copies, waits for them, and re-layouts  4.61 us

profile of v4, /device:TPU:0, one launch (start us, length us, event | category | flops | bytes accessed | tf_op | source)
XLA Modules:
  0.0 58.6 jit_solution(12138117449050388716)
XLA Ops:
  1.3 0.6 %broadcast_in_dim.2.offv_ref = s32[8,128]{1,0:T(8,128)} broadcast(s32[]{:T(128)} %bitcast.11), dimensions={} | broadcast | bytes 4100 | tf_op jit(solution)/shard_map/broadcast_in_dim | solution.py:471
  1.9 52.1 %fused.1 = (f32[2,64,256]{2,1,0:T(8,128)}, f32[2,1024,256]{2,1,0:T(8,128)}) custom-call(s32[8]{0:T(128)} %subs_ref.1, s32[1]{0:T(128)} %copy.12.offset_ref, s32[8,128]{1,0:T(8,128)} %broadcast_in_dim.2.offv_ref, bf16[2,1024,256]{2,1,0:T(8,128)(2,1)} %bitcast.13, s32[1,32768]{1,0:T(1,128)} %bitcast.16, f32[2,1,32768]{2,1,0:T(1,128)} %bitcast.14, ...), custom_call_target="tpu_custom_call" | custom-call | tf_op jit(solution)/shard_map/fused/pallas_call | solution.py:433
  54.0 1.6 %copy.13 = f32[2,1,64,256]{3,2,1,0:T(8,128)} copy(f32[2,1,64,256]{3,2,1,0:T(8,128)} %bitcast.15) | data formatting | bytes 262144
  55.6 3.0 %copy.14 = f32[2,1,1024,256]{3,2,1,0:T(8,128)} copy(f32[2,1,1024,256]{3,2,1,0:T(8,128)} %bitcast.12) | data formatting | bytes 4194304
